TPU v7x, 256 devices: a whole 4x4x8 slice. The times are simulated.
256 devices in a mesh: ctx: 32 (over z, y), head: 8 (over x, core).
Axes of the slice: x: 4, y: 4, z: 8, core: 2. Of those that a mesh axis runs over, the one named last changes fastest.
Arguments:
- queries: bfloat16 [16384, 5120], P('ctx', 'head'), may hold values from -34 to 34
- key_rows: bfloat16 [16384, 5120], P('ctx', 'head'), may hold values from -8 to 8
- value_rows: bfloat16 [16384, 5120], P('ctx', 'head'), may hold values from -23 to 23
- learning_rates: float32 [8, 16384], P('head', 'ctx'), may hold values from 0.02 to 1
- fast_gate: bfloat16 [8, 640, 640], P('head'), may hold values from -0.25 to 0.25
- fast_lift: bfloat16 [8, 640, 640], P('head'), may hold values from -0.25 to 0.25
- fast_down: bfloat16 [8, 640, 640], P('head'), may hold values from -0.25 to 0.25
- output_gain: float32 [5120], P('head'), may hold values from 0.25 to 1.75
- output_weight: bfloat16 [5120, 5120], P(None, 'head'), may hold values from -0.078125 to 0.078125
Outputs:
- layer_output: bfloat16 [16384, 5120], P('ctx', 'head')
All inputs are finite; a program needn't handle non-finite values.
Results may differ from a plain program's by a relative error of at most 0.025.
Values may be sent and summed in bfloat16 or wider, within the bound.
A program may use at most 128 MiB of HBM per device.

v0:
```python
import jax
import jax.numpy as jnp
from jax import lax
from jax.experimental import pallas as pl
from jax.experimental.pallas import tpu as pltpu
from jax.sharding import PartitionSpec as P

HD = 640
ATT_HD = 128
NS_ITERS = 3
TOK = 512
NZ, NY, NX = 8, 4, 4
ROWS = HD // NZ
TOP = 48
TILE = 128
MESH = pl.DeviceIdType.MESH
BF16 = jnp.bfloat16
F32 = jnp.float32

quintic_first = 3.4445
quintic_second = -4.775
quintic_third = 2.0315


def dot(a, b, ca=1, cb=0):
    return lax.dot_general(a, b, (((ca,), (cb,)), ((), ())), preferred_element_type=F32)


def logistic(x):
    return 1.0 / (1.0 + jnp.exp(-x))


def remote(src, dst, send_sem, recv_sem, device):
    return pltpu.make_async_remote_copy(
        src_ref=src, dst_ref=dst, send_sem=send_sem, recv_sem=recv_sem,
        device_id=device, device_id_type=MESH,
    )


def gradient_rows(rows, k, v, rates, wg, wl, wd, hid, scaled, g_gate, g_lift):
    keys = k[rows, :]
    gate_pre = dot(keys, wg[...])
    lift_pre = dot(keys, wl[...])
    sig = logistic(gate_pre)
    silu = gate_pre * sig
    hid[rows, :] = (silu * lift_pre).astype(BF16)
    sc = (rates[rows, :] * v[rows, :].astype(F32)).astype(BF16)
    scaled[rows, :] = sc
    backward = dot(sc, wd[...], 1, 1)
    g_gate[rows, :] = (backward * lift_pre * (sig * (1.0 + gate_pre * (1.0 - sig)))).astype(BF16)
    g_lift[rows, :] = (backward * silu).astype(BF16)


def update_kernel(
    q, k, v, rates, wg, wl, wd,
    att, ren,
    part, rbuf, ybuf, full, kh, vh, pbuf, hid, scaled, g_gate, g_lift, gram, prod, x_it,
    halo_s, halo_r, rs_s, rs_r, y_s, y_r, ag_s, ag_r,
):
    ctx = lax.axis_index("ctx")
    z, y = ctx // NY, ctx % NY
    up = {"ctx": ((z + 1) % NZ) * NY + y}
    down = {"ctx": ((z + NZ - 1) % NZ) * NY + y}
    peers = [{"ctx": z * NY + (y + d) % NY} for d in (1, 2, 3)]
    after = {"ctx": (ctx + 1) % (NZ * NY)}
    before = {"ctx": (ctx + NZ * NY - 1) % (NZ * NY)}
    started = []

    def go(*args):
        copy = remote(*args)
        copy.start()
        started.append(copy)
        return copy

    barrier = pltpu.get_barrier_semaphore()
    everyone = [up, down, after, before] + peers
    for device in everyone:
        pl.semaphore_signal(barrier, inc=1, device_id=device, device_id_type=MESH)
    pl.semaphore_wait(barrier, len(everyone))

    halo_k = go(k, kh, halo_s.at[0], halo_r.at[0], after)
    halo_v = go(v, vh, halo_s.at[1], halo_r.at[1], after)

    @pl.loop(0, TOK // 256)
    def _(i):
        rows = pl.ds(pl.multiple_of(i * 256, 256), 256)
        gradient_rows(rows, k, v, rates, wg, wl, wd, hid, scaled, g_gate, g_lift)

    def block(c, low=0, size=ROWS):
        return pl.ds(pl.multiple_of(((c + 2 * NZ) % NZ) * ROWS + low, 16), size)

    def rs_begin(s):
        go(part.at[s, block(z + 4, 0, TOP)], rbuf.at[s, 0, 0, pl.ds(0, TOP)],
           rs_s.at[s, 0, 0], rs_r.at[s, 0, 0], up)
        go(part.at[s, block(z + 4, TOP, ROWS - TOP)], rbuf.at[s, 1, 0, pl.ds(TOP, ROWS - TOP)],
           rs_s.at[s, 1, 0], rs_r.at[s, 1, 0], down)

    def rs_arrived(s, d, step):
        if step == 1:
            where = rbuf.at[s, d, 0, pl.ds(0, TOP) if d == 0 else pl.ds(TOP, ROWS - TOP)]
        else:
            where = rbuf.at[s, d, step - 1]
        remote(where, where, rs_s.at[s, d, step - 1], rs_r.at[s, d, step - 1],
               up if d == 0 else down).wait_recv()

    def rs_step(s, step):
        for d in (0, 1):
            rs_arrived(s, d, step)
            c = z + 4 - step if d == 0 else z - 4 + step
            spot = rbuf.at[s, d, step - 1]
            if step == 1:
                lo, size = (0, TOP) if d == 0 else (TOP, ROWS - TOP)
                olo, osize = (TOP, ROWS - TOP) if d == 0 else (0, TOP)
                spot[pl.ds(lo, size), :] = (
                    spot[pl.ds(lo, size), :].astype(F32) + part[s, block(c, lo, size), :].astype(F32)
                ).astype(BF16)
                spot[pl.ds(olo, osize), :] = part[s, block(c, olo, osize), :]
            else:
                spot[...] = (spot[...].astype(F32) + part[s, block(c), :].astype(F32)).astype(BF16)
            go(spot, rbuf.at[s, d, step], rs_s.at[s, d, step], rs_r.at[s, d, step],
               up if d == 0 else down)

    def rs_end(s):
        rs_arrived(s, 0, 4)
        rs_arrived(s, 1, 4)
        ybuf[s, y] = (
            part[s, block(z), :].astype(F32) + rbuf[s, 0, 3].astype(F32) + rbuf[s, 1, 3].astype(F32)
        ).astype(BF16)
        for d in range(3):
            go(ybuf.at[s, y], ybuf.at[s, y], y_s.at[s, d], y_r.at[s, d], peers[d])

    def ag_begin(s):
        for d in range(3):
            spot = ybuf.at[s, (y + 3 - d) % NY]
            remote(spot, spot, y_s.at[s, d], y_r.at[s, d], peers[d]).wait_recv()
        total = ybuf[s, 0].astype(F32) + ybuf[s, 1].astype(F32)
        total += ybuf[s, 2].astype(F32) + ybuf[s, 3].astype(F32)
        full[s, block(z), :] = total.astype(BF16)
        spot = full.at[s, block(z)]
        go(spot, spot, ag_s.at[s, 0, 0], ag_r.at[s, 0, 0], up)
        go(spot, spot, ag_s.at[s, 1, 0], ag_r.at[s, 1, 0], down)

    def ag_step(s, step):
        for d in (0, 1):
            c = z - step if d == 0 else z + step
            part_rows = (0, TOP) if d == 0 else (TOP, ROWS - TOP)
            lo, size = part_rows if step == 4 else (0, ROWS)
            spot = full.at[s, block(c, lo, size)]
            remote(spot, spot, ag_s.at[s, d, step - 1], ag_r.at[s, d, step - 1],
                   up if d == 0 else down).wait_recv()
            if step < 4:
                lo, size = part_rows if step == 3 else (0, ROWS)
                spot = full.at[s, block(c, lo, size)]
                go(spot, spot, ag_s.at[s, d, step], ag_r.at[s, d, step], up if d == 0 else down)

    def weights_of(h):
        cols = pl.ds(h * ATT_HD, ATT_HD)
        scale = ATT_HD ** (-0.5)

        @pl.loop(0, TOK // TILE)
        def _(i):
            rows = pl.ds(pl.multiple_of(i * TILE, TILE), TILE)
            own = dot(q[rows, cols], k[:, cols], 1, 1)
            old = dot(q[rows, cols], kh[:, cols], 1, 1)
            row = i * TILE + lax.broadcasted_iota(jnp.int32, (TILE, TOK), 0)
            col = lax.broadcasted_iota(jnp.int32, (TILE, TOK), 1)
            first = jnp.where(ctx == 0, -1e30, 0.0).astype(F32)
            scores = jnp.where(col <= row, own * scale, old * scale + first)
            peak = jnp.max(scores, axis=1, keepdims=True)
            w = jnp.exp(scores - peak)
            total = jnp.sum(w, axis=1, keepdims=True)
            pbuf[h, rows, :] = (w / total).astype(BF16)

    def attend(h):
        cols = pl.ds(h * ATT_HD, ATT_HD)

        @pl.loop(0, TOK // TILE)
        def _(i):
            rows = pl.ds(pl.multiple_of(i * TILE, TILE), TILE)
            w = pbuf[h, rows, :]
            row = i * TILE + lax.broadcasted_iota(jnp.int32, (TILE, TOK), 0)
            col = lax.broadcasted_iota(jnp.int32, (TILE, TOK), 1)
            w_own = jnp.where(col <= row, w, jnp.zeros_like(w))
            w_old = jnp.where(col <= row, jnp.zeros_like(w), w)
            att[rows, cols] = dot(w_own, v[:, cols]) + dot(w_old, vh[:, cols])

    def orthogonalize(s):
        g = full[s].astype(F32)
        size = jnp.sqrt(jnp.sum(jnp.sum(g * g, axis=1, keepdims=True), axis=0, keepdims=True))
        x_it[...] = (g * (1.0 / (size + 1e-06))).astype(BF16)

        @pl.loop(0, NS_ITERS)
        def _(i):
            gram[...] = dot(x_it[...], x_it[...], 1, 1).astype(BF16)
            prod[...] = dot(gram[...], x_it[...]).astype(BF16)
            second = dot(gram[...], prod[...])
            x_it[...] = (
                quintic_first * x_it[...].astype(F32)
                + quintic_second * prod[...].astype(F32)
                + quintic_third * second
            ).astype(BF16)

        initial = (wd, wl, wg)[s][...].astype(F32)
        updated = initial + x_it[...].astype(F32)
        target = jnp.sqrt(jnp.sum(initial * initial, axis=0, keepdims=True))
        current = jnp.sqrt(jnp.sum(updated * updated, axis=0, keepdims=True) + 1e-06)
        ren[s] = (updated * (target / current)).astype(BF16)

    for s, (left, right) in enumerate(((hid, scaled), (k, g_lift), (k, g_gate))):
        part[s] = dot(left[...], right[...], 0, 0).astype(BF16)
        rs_begin(s)
    for step in (1, 2, 3):
        for s in range(3):
            rs_step(s, step)
    halo_k.wait_recv()
    for s in range(3):
        weights_of(s)
        rs_end(s)
    weights_of(3)
    ag_begin(0)
    weights_of(4)
    ag_begin(1)
    ag_begin(2)
    halo_v.wait_recv()
    for step in (1, 2, 3, 4):
        for s in range(3):
            ag_step(s, step)
        attend(step - 1)
    attend(4)
    for s in range(3):
        orthogonalize(s)
    for copy in started:
        copy.wait_send()


def update(queries, key_rows, value_rows, rates, fast_gate, fast_lift, fast_down):
    vmem = pl.BlockSpec(memory_space=pltpu.VMEM)
    dma = pltpu.SemaphoreType.DMA
    square = (HD, HD)
    tokens = (TOK, HD)
    return pl.pallas_call(
        update_kernel,
        name="fast_update",
        out_shape=(jax.ShapeDtypeStruct(tokens, F32), jax.ShapeDtypeStruct((3, HD, HD), BF16)),
        in_specs=[vmem] * 7,
        out_specs=(vmem, vmem),
        scratch_shapes=[
            pltpu.VMEM((3, HD, HD), BF16),
            pltpu.VMEM((3, 2, 4, ROWS, HD), BF16),
            pltpu.VMEM((3, NY, ROWS, HD), BF16),
            pltpu.VMEM((3, HD, HD), BF16),
            pltpu.VMEM(tokens, BF16),
            pltpu.VMEM(tokens, BF16),
            pltpu.VMEM((HD // ATT_HD, TOK, TOK), BF16),
            pltpu.VMEM(tokens, BF16),
            pltpu.VMEM(tokens, BF16),
            pltpu.VMEM(tokens, BF16),
            pltpu.VMEM(tokens, BF16),
            pltpu.VMEM(square, BF16),
            pltpu.VMEM(square, BF16),
            pltpu.VMEM(square, BF16),
            dma((2,)), dma((2,)),
            dma((3, 2, 4)), dma((3, 2, 4)),
            dma((3, 3)), dma((3, 3)),
            dma((3, 2, 4)), dma((3, 2, 4)),
        ],
        compiler_params=pltpu.CompilerParams(
            collective_id=0, has_side_effects=True, vmem_limit_bytes=60 * 1024 * 1024
        ),
    )(queries, key_rows, value_rows, rates, fast_gate, fast_lift, fast_down)


def project_kernel(
    q, att, ren, gain, weight, out,
    cbuf, wbuf, acc, w_sem, d1_s, d1_r, d2_s, d2_r, pr_s, pr_r,
):
    head = lax.axis_index("head")
    x, core = head // 2, head % 2

    def place(offset, other=0):
        side = (core + other) % 2
        return ((x + offset + NX) % NX) * 2 + side

    right, left, partner = ({"head": place(1)}, {"head": place(-1)}, {"head": place(0, 1)})
    started = []

    def go(*args):
        copy = remote(*args)
        copy.start()
        started.append(copy)

    def arrived(spot, send_sem, recv_sem, device):
        remote(spot, spot, send_sem, recv_sem, device).wait_recv()

    order = [place(0), place(0, 1), place(-1), place(1), place(-1, 1), place(1, 1), place(2), place(2, 1)]
    loads = [pltpu.make_async_copy(weight.at[h], wbuf.at[h], w_sem.at[i]) for i, h in enumerate(order)]
    for load in loads:
        load.start()

    barrier = pltpu.get_barrier_semaphore()
    for device in (right, left, partner):
        pl.semaphore_signal(barrier, inc=1, device_id=device, device_id_type=MESH)
    pl.semaphore_wait(barrier, 3)

    def rows_of(t, low=0, size=TILE):
        return pl.ds(t * TILE + low, size)

    chunks = TOK // TILE
    half = TILE // 2
    for t in range(chunks):
        rows = rows_of(t)
        gate = dot(q[rows, :], ren[2])
        lift = dot(q[rows, :], ren[1])
        applied = (gate * logistic(gate) * lift).astype(BF16)
        result = dot(applied, ren[0])
        back = lax.rsqrt(jnp.mean(result * result, axis=1, keepdims=True) + 1e-06)
        cbuf[head, rows, :] = (att[rows, :] + result * back * gain[...]).astype(BF16)
        spot = cbuf.at[head, rows]
        go(spot, spot, d1_s.at[0, t], d1_r.at[0, t], right)
        go(spot, spot, d1_s.at[1, t], d1_r.at[1, t], left)
        go(spot, spot, pr_s.at[0, t], pr_r.at[0, t], partner)

    def add(i, rows, first=False, last=False):
        h = order[i]
        value = dot(cbuf[h, rows, :], wbuf[h])
        if not first:
            value += acc[rows, :]
        if last:
            out[rows, :] = value.astype(BF16)
        else:
            acc[rows, :] = value

    whole = pl.ds(0, TOK)

    def near(t):
        for d in (0, 1):
            h = place(-1) if d == 0 else place(1)
            spot = cbuf.at[h, rows_of(t)]
            arrived(spot, d1_s.at[d, t], d1_r.at[d, t], left if d == 0 else right)
            piece = cbuf.at[h, rows_of(t, d * half, half)]
            go(piece, piece, d2_s.at[d, t], d2_r.at[d, t], right if d == 0 else left)
            go(spot, spot, pr_s.at[1 + d, t], pr_r.at[1 + d, t], partner)

    def far(t):
        h = place(2)
        for d in (0, 1):
            piece = cbuf.at[h, rows_of(t, d * half, half)]
            arrived(piece, d2_s.at[d, t], d2_r.at[d, t], left if d == 0 else right)
        spot = cbuf.at[h, rows_of(t)]
        go(spot, spot, pr_s.at[3, t], pr_r.at[3, t], partner)

    def mirrored(j, t):
        h = place((0, -1, 1, 2)[j], 1)
        spot = cbuf.at[h, rows_of(t)]
        arrived(spot, pr_s.at[j, t], pr_r.at[j, t], partner)

    near(0)
    loads[0].wait()
    add(0, whole, first=True)
    near(1)
    for t in range(chunks):
        mirrored(0, t)
    loads[1].wait()
    add(1, whole)
    near(2)
    near(3)
    far(0)
    loads[2].wait()
    add(2, whole)
    far(1)
    loads[3].wait()
    add(3, whole)
    for t in range(chunks):
        mirrored(1, t)
    loads[4].wait()
    add(4, whole)
    far(2)
    for t in range(chunks):
        mirrored(2, t)
    loads[5].wait()
    add(5, whole)
    loads[6].wait()
    add(6, pl.ds(0, 3 * TILE))
    for t in range(chunks - 1):
        mirrored(3, t)
    loads[7].wait()
    add(7, pl.ds(0, 3 * TILE), last=True)
    far(3)
    add(6, rows_of(3))
    mirrored(3, 3)
    add(7, rows_of(3), last=True)
    for copy in started:
        copy.wait_send()


def project(queries, attended, renewed, gain, weight):
    vmem = pl.BlockSpec(memory_space=pltpu.VMEM)
    dma = pltpu.SemaphoreType.DMA
    heads = 2 * NX
    chunks = TOK // TILE
    return pl.pallas_call(
        project_kernel,
        name="project",
        out_shape=jax.ShapeDtypeStruct((TOK, HD), BF16),
        in_specs=[vmem] * 4 + [pl.BlockSpec(memory_space=pl.ANY)],
        out_specs=vmem,
        scratch_shapes=[
            pltpu.VMEM((heads, TOK, HD), BF16),
            pltpu.VMEM((heads, HD, HD), BF16),
            pltpu.VMEM((TOK, HD), F32),
            dma((heads,)),
            dma((2, chunks)), dma((2, chunks)),
            dma((2, chunks)), dma((2, chunks)),
            dma((4, chunks)), dma((4, chunks)),
        ],
        compiler_params=pltpu.CompilerParams(
            collective_id=1, has_side_effects=True, vmem_limit_bytes=60 * 1024 * 1024
        ),
    )(queries, attended, renewed, gain, weight)


def on_device(
    queries, key_rows, value_rows, learning_rates, fast_gate, fast_lift, fast_down, output_gain, output_weight
):
    attended, renewed = update(
        queries, key_rows, value_rows, jnp.transpose(learning_rates), fast_gate[0], fast_lift[0], fast_down[0]
    )
    return project(
        queries, attended, renewed, output_gain[None], output_weight.reshape(2 * NX, HD, HD)
    )


def solution(mesh):
    return jax.shard_map(
        on_device,
        mesh=mesh,
        in_specs=(
            P("ctx", "head"),
            P("ctx", "head"),
            P("ctx", "head"),
            P("head", "ctx"),
            P("head", None, None),
            P("head", None, None),
            P("head", None, None),
            P("head"),
            P(None, "head"),
        ),
        out_specs=P("ctx", "head"),
        check_vma=False,
    )
```

profile of v0, /device:TPU:1, one launch (start us, length us, event | category | flops | bytes accessed | tf_op | source)
XLA Modules:
  0.0 157.2 jit_solution(12104395531879312934)
XLA Ops:
  0.0 1.3 broadcast_in_dim.3.gain
  1.3 1.5 copy.10.rates
  2.8 117.7 %fast_update.1 = (f32[512,640]{1,0:T(8,128)}, bf16[3,640,640]{2,1,0:T(8,128)(2,1)}) custom-call(bf16[512,640]{1,0:T(8,128)(2,1)} %q.3, bf16[512,640]{1,0:T(8,128)(2,1)} %k.1, bf16[512,640]{1,0:T(8,128)(2,1)} %v.1, f32[512,1]{1,0:T(8,128)} %copy.10.rates, bf16[640,640]{1,0:T(8,128)(2,1)} %bitcast.6, bf16[640,640]{1,0:T(8,128)(2,1)} %bitcast.7, ...), custom_call_target="tpu_custom_call" | custom-call | tf_op jit(solution)/shard_map/fast_update/pallas_call | solution.py:241
  120.5 34.8 %project.1 = bf16[512,640]{1,0:T(8,128)(2,1)} custom-call(bf16[512,640]{1,0:T(8,128)(2,1)} %q.3, f32[512,640]{1,0:T(8,128)} %get-tuple-element.7.att, bf16[3,640,640]{2,1,0:T(8,128)(2,1)} %get-tuple-element.8.ren, f32[1,640]{1,0:T(1,128)} %broadcast_in_dim.3.gain, bf16[8,640,640]{2,1,0:T(8,128)(2,1)} %bitcast.5), custom_call_target="tpu_custom_call" | custom-call | tf_op jit(solution)/shard_map/project/pallas_call | solution.py:401
  155.3 2.0 %copy.12 = bf16[512,640]{1,0:T(8,128)(2,1)} copy(bf16[512,640]{1,0:T(8,128)(2,1)} %project.1) | data formatting | bytes 1310720
where the time goes:
time: 159 us; the launch traced here: 157 us
  Pallas kernels  152 us (96%)
  local copies, waits for them, and re-layouts  4.78 us (3%)
    pallas_call x1, Pallas kernels, update(): pl.pallas_call(update_kernel, name='fast_update', out_shape=(jax.ShapeDty...  118 us
    pallas_call x1, Pallas kernels, project(): pl.pallas_call(project_kernel, name='project', out_shape=jax.ShapeDtypeSt...  34.8 us

commit v1 on v0

v1 whole, which is shorter than its diff:
```python
import math

import jax
import jax.numpy as jnp
from jax import lax
from jax.experimental import pallas as pl
from jax.experimental.pallas import tpu as pltpu
from jax.sharding import PartitionSpec as P

HD = 640
ATT_HD = 128
NS_ITERS = 3
TOK = 512
NZ, NY, NX = 8, 4, 4
ROWS = HD // NZ
TOP = 48
TILE = 128
MESH = pl.DeviceIdType.MESH
BF16 = jnp.bfloat16
F32 = jnp.float32

EXP_SCALE = ATT_HD ** (-0.5) * math.log2(math.e)

quintic_first = 3.4445
quintic_second = -4.775
quintic_third = 2.0315


def dot(a, b, ca=1, cb=0):
    return lax.dot_general(a, b, (((ca,), (cb,)), ((), ())), preferred_element_type=F32)


def logistic(x):
    return 1.0 / (1.0 + jnp.exp(-x))


def remote(src, dst, send_sem, recv_sem, device):
    return pltpu.make_async_remote_copy(
        src_ref=src, dst_ref=dst, send_sem=send_sem, recv_sem=recv_sem,
        device_id=device, device_id_type=MESH,
    )


def gradient_rows(rows, k, v, rates, wg, wl, wd, hid, scaled, g_gate, g_lift):
    keys = k[rows, :]
    gate_pre = dot(keys, wg[...])
    lift_pre = dot(keys, wl[...])
    sig = logistic(gate_pre)
    silu = gate_pre * sig
    hid[rows, :] = (silu * lift_pre).astype(BF16)
    sc = (rates[rows, :1] * v[rows, :].astype(F32)).astype(BF16)
    scaled[rows, :] = sc
    backward = dot(sc, wd[...], 1, 1)
    g_gate[rows, :] = (backward * lift_pre * (sig * (1.0 + gate_pre * (1.0 - sig)))).astype(BF16)
    g_lift[rows, :] = (backward * silu).astype(BF16)


def layer_kernel(
    q, k, v, rates, wg, wl, wd, gain, weight,
    out,
    part, rbuf, ybuf, full, kh, vh, relay, pbuf, hid, scaled, g_gate, g_lift, gram, prod, x_it,
    rate_col, att, ren, cbuf, wbuf, acc,
    halo_s, halo_r, x_s, x_r, rs_s, rs_r, y_s, y_r, ag_s, ag_r,
    w_sem, d1_s, d1_r, d2_s, d2_r, pr_s, pr_r,
):
    ctx = lax.axis_index("ctx")
    z, y = ctx // NY, ctx % NY
    up = {"ctx": ((z + 1) % NZ) * NY + y}
    down = {"ctx": ((z + NZ - 1) % NZ) * NY + y}
    peers = [{"ctx": z * NY + (y + d) % NY} for d in (1, 2, 3)]
    after = {"ctx": z * NY + (y + 1) % NY}
    head = lax.axis_index("head")
    x, core = head // 2, head % 2

    def place(offset, other=0):
        side = (core + other) % 2
        return ((x + offset + NX) % NX) * 2 + side

    right, left, partner = ({"head": place(1)}, {"head": place(-1)}, {"head": place(0, 1)})
    started = []

    def go(*args):
        copy = remote(*args)
        copy.start()
        started.append(copy)
        return copy

    def arrived(spot, send_sem, recv_sem, device):
        remote(spot, spot, send_sem, recv_sem, device).wait_recv()

    order = [place(0), place(0, 1), place(-1), place(1), place(-1, 1), place(1, 1), place(2), place(2, 1)]
    loads = [pltpu.make_async_copy(weight.at[h], wbuf.at[h], w_sem.at[i]) for i, h in enumerate(order)]
    for load in loads:
        load.start()

    barrier = pltpu.get_barrier_semaphore()
    everyone = [up, down, right, left, partner] + peers
    for device in everyone:
        pl.semaphore_signal(barrier, inc=1, device_id=device, device_id_type=MESH)
    pl.semaphore_wait(barrier, len(everyone))

    def piece(p):
        return pl.ds(p * TILE, TILE)

    def mine():
        return pl.ds(pl.multiple_of(y * TILE, TILE), TILE)

    def halo(i, half):
        source, target = ((k, kh), (v, vh))[i]
        rows = pl.ds(half * (TOK // 2), TOK // 2)
        return remote(source.at[rows], target.at[rows], halo_s.at[i, half], halo_r.at[i], after)

    def across(i, p):
        source = (k, v)[i]
        return remote(source.at[piece(p)], relay.at[i, 0], x_s.at[i, p], x_r.at[i, 0], {"ctx": z * NY + p})

    def climb(i, column):
        source, target = ((k, kh), (v, vh))[i]
        if column == 3:
            return remote(source.at[piece(3)], relay.at[i, 1], x_s.at[i, 3], x_r.at[i, 1], up)
        if column == 0:
            return remote(relay.at[i, 0], target.at[piece(0)], x_s.at[i, 3], halo_r.at[i], up)
        return remote(relay.at[i, 0], relay.at[i, 1], x_s.at[i, 3], x_r.at[i, 1], up)

    def land(i):
        target = (kh, vh)[i]
        return remote(relay.at[i, 1], target.at[mine()], x_s.at[i, 4], halo_r.at[i], {"ctx": z * NY})

    def halo_begin(i):
        @pl.when(y == 3)
        def _():
            for p in range(3):
                across(i, p).start()
            climb(i, 3).start()

    def halo_half(i, half):
        @pl.when(y != 3)
        def _():
            halo(i, half).start()

    def halo_climb(i):
        @pl.when(y != 3)
        def _():
            across(i, 0).wait_recv()

        @pl.when(y == 0)
        def _():
            climb(i, 0).start()

        @pl.when((y == 1) | (y == 2))
        def _():
            climb(i, 1).start()

    def halo_land(i):
        @pl.when(y != 0)
        def _():
            climb(i, 1).wait_recv()
            land(i).start()

    def halo_wait(i):
        target = (kh, vh)[i]
        remote(target, target, halo_s.at[i, 0], halo_r.at[i], after).wait_recv()

    def halo_sent(i):
        climb(i, 1).wait_send()

        @pl.when(y == 3)
        def _():
            for p in range(3):
                across(i, p).wait_send()

        @pl.when(y != 3)
        def _():
            halo(i, 0).wait_send()
            halo(i, 1).wait_send()

        @pl.when(y != 0)
        def _():
            land(i).wait_send()

    halo_begin(0)
    halo_half(0, 0)
    halo_half(0, 1)

    rate_col[...] = jnp.transpose(jnp.broadcast_to(rates[...], (TILE, TOK)))

    @pl.loop(0, TOK // 256)
    def _(i):
        rows = pl.ds(pl.multiple_of(i * 256, 256), 256)
        gradient_rows(rows, k, v, rate_col, wg, wl, wd, hid, scaled, g_gate, g_lift)

    def block(c, low=0, size=ROWS):
        return pl.ds(pl.multiple_of(((c + 2 * NZ) % NZ) * ROWS + low, 16), size)

    def rs_begin(s):
        go(part.at[s, block(z + 4, 0, TOP)], rbuf.at[s, 0, 0, pl.ds(0, TOP)],
           rs_s.at[s, 0, 0], rs_r.at[s, 0, 0], up)
        go(part.at[s, block(z + 4, TOP, ROWS - TOP)], rbuf.at[s, 1, 0, pl.ds(TOP, ROWS - TOP)],
           rs_s.at[s, 1, 0], rs_r.at[s, 1, 0], down)

    def rs_arrived(s, d, step):
        if step == 1:
            where = rbuf.at[s, d, 0, pl.ds(0, TOP) if d == 0 else pl.ds(TOP, ROWS - TOP)]
        else:
            where = rbuf.at[s, d, step - 1]
        remote(where, where, rs_s.at[s, d, step - 1], rs_r.at[s, d, step - 1],
               up if d == 0 else down).wait_recv()

    def rs_step(s, step):
        for d in (0, 1):
            rs_arrived(s, d, step)
            c = z + 4 - step if d == 0 else z - 4 + step
            spot = rbuf.at[s, d, step - 1]
            if step == 1:
                lo, size = (0, TOP) if d == 0 else (TOP, ROWS - TOP)
                olo, osize = (TOP, ROWS - TOP) if d == 0 else (0, TOP)
                spot[pl.ds(lo, size), :] = (
                    spot[pl.ds(lo, size), :].astype(F32) + part[s, block(c, lo, size), :].astype(F32)
                ).astype(BF16)
                spot[pl.ds(olo, osize), :] = part[s, block(c, olo, osize), :]
            else:
                spot[...] = (spot[...].astype(F32) + part[s, block(c), :].astype(F32)).astype(BF16)
            go(spot, rbuf.at[s, d, step], rs_s.at[s, d, step], rs_r.at[s, d, step],
               up if d == 0 else down)

    def rs_end(s):
        rs_arrived(s, 0, 4)
        rs_arrived(s, 1, 4)
        ybuf[s, y] = (
            part[s, block(z), :].astype(F32) + rbuf[s, 0, 3].astype(F32) + rbuf[s, 1, 3].astype(F32)
        ).astype(BF16)
        for d in range(3):
            go(ybuf.at[s, y], ybuf.at[s, y], y_s.at[s, d], y_r.at[s, d], peers[d])

    def ag_begin(s):
        for d in range(3):
            spot = ybuf.at[s, (y + 3 - d) % NY]
            remote(spot, spot, y_s.at[s, d], y_r.at[s, d], peers[d]).wait_recv()
        total = ybuf[s, 0].astype(F32) + ybuf[s, 1].astype(F32)
        total += ybuf[s, 2].astype(F32) + ybuf[s, 3].astype(F32)
        full[s, block(z), :] = total.astype(BF16)
        spot = full.at[s, block(z)]
        go(spot, spot, ag_s.at[s, 0, 0], ag_r.at[s, 0, 0], up)
        go(spot, spot, ag_s.at[s, 1, 0], ag_r.at[s, 1, 0], down)

    def ag_step(s, step):
        for d in (0, 1):
            c = z - step if d == 0 else z + step
            part_rows = (0, TOP) if d == 0 else (TOP, ROWS - TOP)
            lo, size = part_rows if step == 4 else (0, ROWS)
            spot = full.at[s, block(c, lo, size)]
            remote(spot, spot, ag_s.at[s, d, step - 1], ag_r.at[s, d, step - 1],
                   up if d == 0 else down).wait_recv()
            if step < 4:
                lo, size = part_rows if step == 3 else (0, ROWS)
                spot = full.at[s, block(c, lo, size)]
                go(spot, spot, ag_s.at[s, d, step], ag_r.at[s, d, step], up if d == 0 else down)

    def rows_of(t, low=0, size=TILE):
        return pl.ds(t * TILE + low, size)

    def own_keys():
        row = lax.broadcasted_iota(jnp.int32, (TILE, TILE), 0)
        return lax.broadcasted_iota(jnp.int32, (TILE, TILE), 1) <= row

    def head_columns(h):
        return pl.ds(pl.multiple_of(h * ATT_HD, ATT_HD), ATT_HD)

    def weights_of(t):
        rows, low, high = rows_of(t), t * TILE, (t + 1) * TILE

        @pl.loop(0, HD // ATT_HD)
        def _(h):
            cols = head_columns(h)
            first = jnp.where(ctx == 0, -1e30, 0.0).astype(F32)
            own = dot(q[rows, cols], k[pl.ds(0, high), cols], 1, 1)
            old = dot(q[rows, cols], kh[pl.ds(low, TOK - low), cols], 1, 1) + first
            blocks = [own[:, :low]] if t else []
            blocks.append(jnp.where(own_keys(), own[:, low:], old[:, :TILE]))
            if high < TOK:
                blocks.append(old[:, TILE:])
            scores = jnp.concatenate(blocks, axis=1)
            peak = jnp.max(scores, axis=1, keepdims=True)
            w = jnp.exp2((scores - peak) * EXP_SCALE)
            total = jnp.sum(w, axis=1, keepdims=True)
            pbuf[h, rows, :] = (w * (1.0 / total)).astype(BF16)

    def attend(t):
        rows, low, high = rows_of(t), t * TILE, (t + 1) * TILE

        @pl.loop(0, HD // ATT_HD)
        def _(h):
            cols = head_columns(h)
            diagonal = pbuf[h, rows, pl.ds(low, TILE)]
            zero = jnp.zeros_like(diagonal)
            value = dot(jnp.where(own_keys(), diagonal, zero), v[pl.ds(low, TILE), cols])
            value += dot(jnp.where(own_keys(), zero, diagonal), vh[pl.ds(low, TILE), cols])
            if t:
                value += dot(pbuf[h, rows, pl.ds(0, low)], v[pl.ds(0, low), cols])
            if high < TOK:
                value += dot(pbuf[h, rows, pl.ds(high, TOK - high)], vh[pl.ds(high, TOK - high), cols])
            att[rows, cols] = value

    def normalize(s):
        g = full[s].astype(F32)
        size = jnp.sqrt(jnp.sum(jnp.sum(g * g, axis=1, keepdims=True), axis=0, keepdims=True))
        x_it[...] = (g * (1.0 / (size + 1e-06))).astype(BF16)

    def iterate():
        gram[...] = dot(x_it[...], x_it[...], 1, 1).astype(BF16)
        prod[...] = dot(gram[...], x_it[...]).astype(BF16)
        second = dot(gram[...], prod[...])
        x_it[...] = (
            quintic_first * x_it[...].astype(F32)
            + quintic_second * prod[...].astype(F32)
            + quintic_third * second
        ).astype(BF16)

    def renew(s):
        initial = (wd, wl, wg)[s][...].astype(F32)
        updated = initial + x_it[...].astype(F32)
        target = jnp.sqrt(jnp.sum(initial * initial, axis=0, keepdims=True))
        current = jnp.sqrt(jnp.sum(updated * updated, axis=0, keepdims=True) + 1e-06)
        ren[s] = (updated * (target / current)).astype(BF16)

    def gradient(s):
        left, right = ((hid, scaled), (k, g_lift), (k, g_gate))[s]
        part[s] = dot(left[...], right[...], 0, 0).astype(BF16)

    gradient(0)
    rs_begin(0)
    gradient(1)
    rs_begin(1)
    gradient(2)
    rs_step(0, 1)
    rs_step(1, 1)
    rs_begin(2)
    halo_climb(0)
    rs_step(0, 2)
    rs_step(1, 2)
    rs_step(2, 1)
    halo_land(0)
    rs_step(0, 3)
    rs_step(1, 3)
    rs_step(2, 2)
    rs_end(0)
    rs_end(1)
    halo_wait(0)
    weights_of(0)
    rs_step(2, 3)
    ag_begin(0)
    weights_of(1)
    ag_begin(1)
    rs_end(2)
    halo_begin(1)
    halo_half(1, 0)
    halo_half(1, 1)
    weights_of(2)
    ag_step(0, 1)
    ag_step(1, 1)
    weights_of(3)
    ag_begin(2)
    halo_climb(1)
    ag_step(0, 2)
    ag_step(1, 2)
    ag_step(2, 1)
    halo_land(1)
    ag_step(0, 3)
    ag_step(1, 3)
    ag_step(2, 2)
    ag_step(0, 4)
    normalize(0)
    iterate()
    ag_step(2, 3)
    iterate()
    ag_step(1, 4)
    iterate()
    renew(0)
    for s in (1, 2):
        if s == 2:
            ag_step(2, 4)
        normalize(s)
        pl.loop(0, NS_ITERS)(lambda i: iterate())
        renew(s)
    halo_wait(1)

    chunks = TOK // TILE
    half = TILE // 2
    for t in range(chunks):
        attend(t)
        rows = rows_of(t)
        gate = dot(q[rows, :], ren[2])
        lift = dot(q[rows, :], ren[1])
        applied = (gate * logistic(gate) * lift).astype(BF16)
        result = dot(applied, ren[0])
        back = lax.rsqrt(jnp.mean(result * result, axis=1, keepdims=True) + 1e-06)
        cbuf[head, rows, :] = (att[rows, :] + result * back * gain[...][None, :]).astype(BF16)
        spot = cbuf.at[head, rows]
        go(spot, spot, d1_s.at[0, t], d1_r.at[0, t], right)
        go(spot, spot, d1_s.at[1, t], d1_r.at[1, t], left)
        go(spot, spot, pr_s.at[0, t], pr_r.at[0, t], partner)

    def add(i, rows, first=False, last=False):
        h = order[i]
        value = dot(cbuf[h, rows, :], wbuf[h])
        if not first:
            value += acc[rows, :]
        if last:
            out[rows, :] = value.astype(BF16)
        else:
            acc[rows, :] = value

    whole = pl.ds(0, TOK)

    def near(t):
        for d in (0, 1):
            h = place(-1) if d == 0 else place(1)
            spot = cbuf.at[h, rows_of(t)]
            arrived(spot, d1_s.at[d, t], d1_r.at[d, t], left if d == 0 else right)
            piece = cbuf.at[h, rows_of(t, d * half, half)]
            go(piece, piece, d2_s.at[d, t], d2_r.at[d, t], right if d == 0 else left)
            go(spot, spot, pr_s.at[1 + d, t], pr_r.at[1 + d, t], partner)

    def far(t):
        h = place(2)
        for d in (0, 1):
            piece = cbuf.at[h, rows_of(t, d * half, half)]
            arrived(piece, d2_s.at[d, t], d2_r.at[d, t], left if d == 0 else right)
        spot = cbuf.at[h, rows_of(t)]
        go(spot, spot, pr_s.at[3, t], pr_r.at[3, t], partner)

    def mirrored(j, t):
        h = place((0, -1, 1, 2)[j], 1)
        spot = cbuf.at[h, rows_of(t)]
        arrived(spot, pr_s.at[j, t], pr_r.at[j, t], partner)

    near(0)
    loads[0].wait()
    add(0, whole, first=True)
    near(1)
    for t in range(chunks):
        mirrored(0, t)
    loads[1].wait()
    add(1, whole)
    near(2)
    near(3)
    far(0)
    loads[2].wait()
    add(2, whole)
    far(1)
    loads[3].wait()
    add(3, whole)
    for t in range(chunks):
        mirrored(1, t)
    loads[4].wait()
    add(4, whole)
    far(2)
    for t in range(chunks):
        mirrored(2, t)
    loads[5].wait()
    add(5, whole)
    loads[6].wait()
    add(6, pl.ds(0, 3 * TILE))
    for t in range(chunks - 1):
        mirrored(3, t)
    loads[7].wait()
    add(7, pl.ds(0, 3 * TILE), last=True)
    far(3)
    add(6, rows_of(3))
    mirrored(3, 3)
    add(7, rows_of(3), last=True)
    for copy in started:
        copy.wait_send()
    halo_sent(0)
    halo_sent(1)


def layer(queries, key_rows, value_rows, rates, fast_gate, fast_lift, fast_down, gain, weight):
    vmem = pl.BlockSpec(memory_space=pltpu.VMEM)
    dma = pltpu.SemaphoreType.DMA
    square = (HD, HD)
    tokens = (TOK, HD)
    heads = 2 * NX
    chunks = TOK // TILE
    return pl.pallas_call(
        layer_kernel,
        name="layer",
        out_shape=jax.ShapeDtypeStruct(tokens, BF16),
        in_specs=[vmem] * 8 + [pl.BlockSpec(memory_space=pl.ANY)],
        out_specs=vmem,
        scratch_shapes=[
            pltpu.VMEM((3, HD, HD), BF16),
            pltpu.VMEM((3, 2, 4, ROWS, HD), BF16),
            pltpu.VMEM((3, NY, ROWS, HD), BF16),
            pltpu.VMEM((3, HD, HD), BF16),
            pltpu.VMEM(tokens, BF16),
            pltpu.VMEM(tokens, BF16),
            pltpu.VMEM((2, 2, TILE, HD), BF16),
            pltpu.VMEM((HD // ATT_HD, TOK, TOK), BF16),
            pltpu.VMEM(tokens, BF16),
            pltpu.VMEM(tokens, BF16),
            pltpu.VMEM(tokens, BF16),
            pltpu.VMEM(tokens, BF16),
            pltpu.VMEM(square, BF16),
            pltpu.VMEM(square, BF16),
            pltpu.VMEM(square, BF16),
            pltpu.VMEM((TOK, TILE), F32),
            pltpu.VMEM(tokens, F32),
            pltpu.VMEM((3, HD, HD), BF16),
            pltpu.VMEM((heads, TOK, HD), BF16),
            pltpu.VMEM((heads, HD, HD), BF16),
            pltpu.VMEM(tokens, F32),
            dma((2, 2)), dma((2,)),
            dma((2, 5)), dma((2, 2)),
            dma((3, 2, 4)), dma((3, 2, 4)),
            dma((3, 3)), dma((3, 3)),
            dma((3, 2, 4)), dma((3, 2, 4)),
            dma((heads,)),
            dma((2, chunks)), dma((2, chunks)),
            dma((2, chunks)), dma((2, chunks)),
            dma((4, chunks)), dma((4, chunks)),
        ],
        compiler_params=pltpu.CompilerParams(
            collective_id=0, has_side_effects=True, vmem_limit_bytes=60 * 1024 * 1024
        ),
    )(queries, key_rows, value_rows, rates, fast_gate, fast_lift, fast_down, gain, weight)


def on_device(
    queries, key_rows, value_rows, learning_rates, fast_gate, fast_lift, fast_down, output_gain, output_weight
):
    return layer(
        queries, key_rows, value_rows, learning_rates, fast_gate[0], fast_lift[0], fast_down[0],
        output_gain, output_weight.reshape(2 * NX, HD, HD),
    )


def solution(mesh):
    return jax.shard_map(
        on_device,
        mesh=mesh,
        in_specs=(
            P("ctx", "head"),
            P("ctx", "head"),
            P("ctx", "head"),
            P("head", "ctx"),
            P("head", None, None),
            P("head", None, None),
            P("head", None, None),
            P("head"),
            P(None, "head"),
        ),
        out_specs=P("ctx", "head"),
        check_vma=False,
    )
```

time: 159 us -> 123 us (0.77)
  Pallas kernels: 152 us -> 121 us
  local copies, waits for them, and re-layouts: 4.78 us -> 1.98 us
    pallas_call x2 -> x1, Pallas kernels: 152 us -> 121 us  [layer(): pl.pallas_call(layer_kernel, name='layer', out_shape=jax.ShapeDtypeStruct...]
where the time goes in v1:
time: 123 us
  Pallas kernels  121 us (98%)
  local copies, waits for them, and re-layouts  1.98 us (2%)
    pallas_call x1, Pallas kernels, layer(): pl.pallas_call(layer_kernel, name='layer', out_shape=jax.ShapeDtypeStruct...  121 us

profile of v1, /device:TPU:1, one launch (start us, length us, event | category | flops | bytes accessed | tf_op | source)
XLA Modules:
  0.0 122.7 jit_solution(15032576992442641461)
XLA Ops:
  0.0 120.8 %layer.1 = bf16[512,640]{1,0:T(8,128)(2,1)} custom-call(bf16[512,640]{1,0:T(8,128)(2,1)} %q.1, bf16[512,640]{1,0:T(8,128)(2,1)} %k.1, bf16[512,640]{1,0:T(8,128)(2,1)} %v.1, f32[1,512]{1,0:T(1,128)} %rates.1, bf16[640,640]{1,0:T(8,128)(2,1)} %bitcast.5, bf16[640,640]{1,0:T(8,128)(2,1)} %bitcast.6, bf16[640,640]{1,0:T(8,128)(2,1)} %bitcast.7, f32[640]{0:T(1024)} %gain.1, ...), custom_call_target="tpu_custom_call" | custom-call | tf_op jit(solution)/shard_map/layer/pallas_call | solution.py:485
  120.8 2.0 %copy.11 = bf16[512,640]{1,0:T(8,128)(2,1)} copy(bf16[512,640]{1,0:T(8,128)(2,1)} %layer.1) | data formatting | bytes 1310720

commit v2 on v1

--- a/solution.py
+++ b/solution.py
@@ -59,9 +59,9 @@
     q, k, v, rates, wg, wl, wd, gain, weight,
     out,
     part, rbuf, ybuf, full, kh, vh, relay, pbuf, hid, scaled, g_gate, g_lift, gram, prod, x_it,
-    rate_col, att, ren, cbuf, wbuf, acc,
+    rate_col, att, ren, cbuf, wown, wbuf, acc, acc_other, o_out, o_in,
     halo_s, halo_r, x_s, x_r, rs_s, rs_r, y_s, y_r, ag_s, ag_r,
-    w_sem, d1_s, d1_r, d2_s, d2_r, pr_s, pr_r,
+    w_sem, wx_s, wx_r, d1_s, d1_r, d2_s, d2_r, pr_s, pr_r, o_s, o_r,
 ):
     ctx = lax.axis_index("ctx")
     z, y = ctx // NY, ctx % NY
@@ -88,13 +88,15 @@
     def arrived(spot, send_sem, recv_sem, device):
         remote(spot, spot, send_sem, recv_sem, device).wait_recv()
 
-    order = [place(0), place(0, 1), place(-1), place(1), place(-1, 1), place(1, 1), place(2), place(2, 1)]
-    loads = [pltpu.make_async_copy(weight.at[h], wbuf.at[h], w_sem.at[i]) for i, h in enumerate(order)]
-    for load in loads:
-        load.start()
+    def chip(offset):
+        return (x + offset + NX) % NX
+
+    order = [head, place(0, 1)] + [chip(offset) * 2 + p for offset in (-1, 1, 2) for p in (0, 1)]
+    loads = [pltpu.make_async_copy(weight.at[h], wown.at[h], w_sem.at[i]) for i, h in enumerate(order)]
 
     barrier = pltpu.get_barrier_semaphore()
-    everyone = [up, down, right, left, partner] + peers
+    sides = [{"head": chip(offset) * 2 + p} for offset in (-1, 1) for p in (0, 1)]
+    everyone = [up, down, partner] + peers + sides
     for device in everyone:
         pl.semaphore_signal(barrier, inc=1, device_id=device, device_id_type=MESH)
     pl.semaphore_wait(barrier, len(everyone))
@@ -182,6 +184,10 @@
     halo_half(0, 0)
     halo_half(0, 1)
 
+    for h in range(2 * NX):
+        go(weight.at[h], wbuf.at[h], wx_s.at[h], wx_r.at[h], partner)
+    for load in loads:
+        load.start()
     rate_col[...] = jnp.transpose(jnp.broadcast_to(rates[...], (TILE, TOK)))
 
     @pl.loop(0, TOK // 256)
@@ -266,10 +272,10 @@
     def head_columns(h):
         return pl.ds(pl.multiple_of(h * ATT_HD, ATT_HD), ATT_HD)
 
-    def weights_of(t):
+    def weights_of(t, begin=0, end=HD // ATT_HD):
         rows, low, high = rows_of(t), t * TILE, (t + 1) * TILE
 
-        @pl.loop(0, HD // ATT_HD)
+        @pl.loop(begin, end)
         def _(h):
             cols = head_columns(h)
             first = jnp.where(ctx == 0, -1e30, 0.0).astype(F32)
@@ -330,63 +336,72 @@
     gradient(0)
     rs_begin(0)
     gradient(1)
-    rs_begin(1)
     gradient(2)
     rs_step(0, 1)
+    rs_begin(1)
+    rs_begin(2)
+    rs_step(0, 2)
     rs_step(1, 1)
-    rs_begin(2)
+    rs_step(2, 1)
     halo_climb(0)
-    rs_step(0, 2)
+    rs_step(0, 3)
     rs_step(1, 2)
-    rs_step(2, 1)
+    rs_step(2, 2)
     halo_land(0)
-    rs_step(0, 3)
+    rs_end(0)
     rs_step(1, 3)
-    rs_step(2, 2)
-    rs_end(0)
+    rs_step(2, 3)
     rs_end(1)
     halo_wait(0)
-    weights_of(0)
-    rs_step(2, 3)
+    weights_of(0, 0, 3)
     ag_begin(0)
-    weights_of(1)
-    ag_begin(1)
+    weights_of(0, 3, 5)
     rs_end(2)
     halo_begin(1)
     halo_half(1, 0)
     halo_half(1, 1)
-    weights_of(2)
+    weights_of(1, 0, 3)
     ag_step(0, 1)
+    weights_of(1, 3, 5)
+    ag_begin(1)
+    weights_of(2, 0, 3)
+    ag_step(0, 2)
+    halo_climb(1)
+    weights_of(2, 3, 5)
+    ag_begin(2)
+    weights_of(3, 0, 3)
     ag_step(1, 1)
-    weights_of(3)
-    ag_begin(2)
-    halo_climb(1)
-    ag_step(0, 2)
+    weights_of(3, 3, 5)
+    ag_step(0, 3)
+    ag_step(2, 1)
     ag_step(1, 2)
-    ag_step(2, 1)
-    halo_land(1)
-    ag_step(0, 3)
-    ag_step(1, 3)
-    ag_step(2, 2)
     ag_step(0, 4)
     normalize(0)
     iterate()
+    ag_step(2, 2)
+    iterate()
+    ag_step(1, 3)
+    halo_land(1)
+    iterate()
     ag_step(2, 3)
-    iterate()
+    renew(0)
     ag_step(1, 4)
-    iterate()
-    renew(0)
-    for s in (1, 2):
-        if s == 2:
-            ag_step(2, 4)
-        normalize(s)
-        pl.loop(0, NS_ITERS)(lambda i: iterate())
-        renew(s)
+    normalize(1)
+    iterate()
+    ag_step(2, 4)
+    iterate()
+    iterate()
+    renew(1)
+    normalize(2)
+    iterate()
+    iterate()
+    iterate()
+    renew(2)
     halo_wait(1)
 
     chunks = TOK // TILE
     half = TILE // 2
-    for t in range(chunks):
+    for t in (0, 2, 1, 3):
         attend(t)
         rows = rows_of(t)
         gate = dot(q[rows, :], ren[2])
@@ -396,81 +411,81 @@
         back = lax.rsqrt(jnp.mean(result * result, axis=1, keepdims=True) + 1e-06)
         cbuf[head, rows, :] = (att[rows, :] + result * back * gain[...][None, :]).astype(BF16)
         spot = cbuf.at[head, rows]
-        go(spot, spot, d1_s.at[0, t], d1_r.at[0, t], right)
-        go(spot, spot, d1_s.at[1, t], d1_r.at[1, t], left)
-        go(spot, spot, pr_s.at[0, t], pr_r.at[0, t], partner)
-
-    def add(i, rows, first=False, last=False):
+        side, c = t // 2, t % 2
+        go(spot, spot, d1_s.at[0, t], d1_r.at[0, core, c], {"head": chip(1) * 2 + side})
+        go(spot, spot, d1_s.at[1, t], d1_r.at[1, core, c], {"head": chip(-1) * 2 + side})
+
+        @pl.when(core != side)
+        def _():
+            remote(spot, spot, pr_s.at[c], pr_r.at[c], partner).start()
+
+    def here(c, low=0, size=TILE):
+        return pl.ds(pl.multiple_of(core * 2 * TILE + c * TILE + low, half), size)
+
+    def near(c):
+        for p in (0, 1):
+            for d in (0, 1):
+                h = chip(2 * d - 1) * 2 + p
+                spot = cbuf.at[h, here(c)]
+                arrived(spot, d1_s.at[d, 0], d1_r.at[d, p, c], left if d == 0 else right)
+                piece = cbuf.at[h, here(c, d * half, half)]
+                go(piece, piece, d2_s.at[d, p, c], d2_r.at[d, p, c], right if d == 0 else left)
+
+    def far(p, c):
+        for d in (0, 1):
+            piece = cbuf.at[chip(2) * 2 + p, here(c, d * half, half)]
+            arrived(piece, d2_s.at[d, p, c], d2_r.at[d, p, c], left if d == 0 else right)
+
+    def mirrored(c):
+        spot = cbuf.at[place(0, 1), here(c)]
+        arrived(spot, pr_s.at[c], pr_r.at[c], partner)
+
+    def add(i, c=None, first=False, last=False):
         h = order[i]
-        value = dot(cbuf[h, rows, :], wbuf[h])
-        if not first:
-            value += acc[rows, :]
-        if last:
-            out[rows, :] = value.astype(BF16)
-        else:
-            acc[rows, :] = value
-
-    whole = pl.ds(0, TOK)
-
-    def near(t):
-        for d in (0, 1):
-            h = place(-1) if d == 0 else place(1)
-            spot = cbuf.at[h, rows_of(t)]
-            arrived(spot, d1_s.at[d, t], d1_r.at[d, t], left if d == 0 else right)
-            piece = cbuf.at[h, rows_of(t, d * half, half)]
-            go(piece, piece, d2_s.at[d, t], d2_r.at[d, t], right if d == 0 else left)
-            go(spot, spot, pr_s.at[1 + d, t], pr_r.at[1 + d, t], partner)
-
-    def far(t):
-        h = place(2)
-        for d in (0, 1):
-            piece = cbuf.at[h, rows_of(t, d * half, half)]
-            arrived(piece, d2_s.at[d, t], d2_r.at[d, t], left if d == 0 else right)
-        spot = cbuf.at[h, rows_of(t)]
-        go(spot, spot, pr_s.at[3, t], pr_r.at[3, t], partner)
-
-    def mirrored(j, t):
-        h = place((0, -1, 1, 2)[j], 1)
-        spot = cbuf.at[h, rows_of(t)]
-        arrived(spot, pr_s.at[j, t], pr_r.at[j, t], partner)
-
+        rows = pl.ds(core * 2 * TILE, 2 * TILE) if c is None else here(c)
+        spot = pl.ds(0, 2 * TILE) if c is None else pl.ds(c * TILE, TILE)
+        tokens = cbuf[h, rows, :]
+        for matrix, total, result in ((wbuf, acc_other, o_out), (wown, acc, None)):
+            value = dot(tokens, matrix[h])
+            if not first:
+                value += total[spot, :]
+            if not last:
+                total[spot, :] = value
+            elif result is None:
+                out[rows, :] = value.astype(BF16)
+            else:
+                result[spot, :] = value.astype(BF16)
+                go(o_out.at[spot], o_in.at[spot], o_s.at[c], o_r.at[c], partner)
+
+    def weights_here(i):
+        h = order[i]
+        loads[i].wait()
+        arrived(wbuf.at[h], wx_s.at[h], wx_r.at[h], partner)
+
+    for i in range(2 * NX):
+        weights_here(i)
     near(0)
-    loads[0].wait()
-    add(0, whole, first=True)
+    add(0, first=True)
+    for c in (0, 1):
+        mirrored(c)
+    add(1)
     near(1)
-    for t in range(chunks):
-        mirrored(0, t)
-    loads[1].wait()
-    add(1, whole)
-    near(2)
-    near(3)
-    far(0)
-    loads[2].wait()
-    add(2, whole)
-    far(1)
-    loads[3].wait()
-    add(3, whole)
-    for t in range(chunks):
-        mirrored(1, t)
-    loads[4].wait()
-    add(4, whole)
-    far(2)
-    for t in range(chunks):
-        mirrored(2, t)
-    loads[5].wait()
-    add(5, whole)
-    loads[6].wait()
-    add(6, pl.ds(0, 3 * TILE))
-    for t in range(chunks - 1):
-        mirrored(3, t)
-    loads[7].wait()
-    add(7, pl.ds(0, 3 * TILE), last=True)
-    far(3)
-    add(6, rows_of(3))
-    mirrored(3, 3)
-    add(7, rows_of(3), last=True)
+    for i in (2, 3, 4, 5):
+        add(i)
+    for c in (0, 1):
+        for p in (0, 1):
+            far(p, c)
+            add(6 + p, c, last=p == 1)
+    other = pl.ds(pl.multiple_of((1 - core) * 2 * TILE, 2 * TILE), 2 * TILE)
+    for c in (0, 1):
+        spot = o_in.at[pl.ds(c * TILE, TILE)]
+        arrived(spot, o_s.at[c], o_r.at[c], partner)
+    out[other, :] = o_in[...]
     for copy in started:
         copy.wait_send()
+    for c in (0, 1):
+        spot = cbuf.at[head, rows_of(c)]
+        remote(spot, spot, pr_s.at[c], pr_r.at[c], partner).wait_send()
     halo_sent(0)
     halo_sent(1)
 
@@ -509,16 +524,22 @@
             pltpu.VMEM((3, HD, HD), BF16),
             pltpu.VMEM((heads, TOK, HD), BF16),
             pltpu.VMEM((heads, HD, HD), BF16),
-            pltpu.VMEM(tokens, F32),
+            pltpu.VMEM((heads, HD, HD), BF16),
+            pltpu.VMEM((TOK // 2, HD), F32),
+            pltpu.VMEM((TOK // 2, HD), F32),
+            pltpu.VMEM((TOK // 2, HD), BF16),
+            pltpu.VMEM((TOK // 2, HD), BF16),
             dma((2, 2)), dma((2,)),
             dma((2, 5)), dma((2, 2)),
             dma((3, 2, 4)), dma((3, 2, 4)),
             dma((3, 3)), dma((3, 3)),
             dma((3, 2, 4)), dma((3, 2, 4)),
             dma((heads,)),
-            dma((2, chunks)), dma((2, chunks)),
-            dma((2, chunks)), dma((2, chunks)),
-            dma((4, chunks)), dma((4, chunks)),
+            dma((heads,)), dma((heads,)),
+            dma((2, chunks)), dma((2, 2, 2)),
+            dma((2, 2, 2)), dma((2, 2, 2)),
+            dma((2,)), dma((2,)),
+            dma((2,)), dma((2,)),
         ],
         compiler_params=pltpu.CompilerParams(
             collective_id=0, has_side_effects=True, vmem_limit_bytes=60 * 1024 * 1024

time: 123 us -> 123 us (level)
  no operation moved by 1% of the time
where the time goes in v2:
time: 123 us; the launch traced here: 122 us
  Pallas kernels  121 us (98%)
  local copies, waits for them, and re-layouts  1.98 us (2%)
    pallas_call x1, Pallas kernels, layer(): pl.pallas_call(layer_kernel, name='layer', out_shape=jax.ShapeDtypeStruct...  121 us

profile of v2, /device:TPU:1, one launch (start us, length us, event | category | flops | bytes accessed | tf_op | source)
XLA Modules:
  0.0 122.5 jit_solution(12881213787941915350)
XLA Ops:
  0.0 120.5 %layer.1 = bf16[512,640]{1,0:T(8,128)(2,1)} custom-call(bf16[512,640]{1,0:T(8,128)(2,1)} %q.1, bf16[512,640]{1,0:T(8,128)(2,1)} %k.1, bf16[512,640]{1,0:T(8,128)(2,1)} %v.1, f32[1,512]{1,0:T(1,128)} %rates.1, bf16[640,640]{1,0:T(8,128)(2,1)} %bitcast.5, bf16[640,640]{1,0:T(8,128)(2,1)} %bitcast.6, bf16[640,640]{1,0:T(8,128)(2,1)} %bitcast.7, f32[640]{0:T(1024)} %gain.1, ...), custom_call_target="tpu_custom_call" | custom-call | tf_op jit(solution)/shard_map/layer/pallas_call | solution.py:500
  120.5 2.0 %copy.11 = bf16[512,640]{1,0:T(8,128)(2,1)} copy(bf16[512,640]{1,0:T(8,128)(2,1)} %layer.1) | data formatting | bytes 1310720

commit v3 on v2

--- a/solution.py
+++ b/solution.py
@@ -184,10 +184,6 @@
     halo_half(0, 0)
     halo_half(0, 1)
 
-    for h in range(2 * NX):
-        go(weight.at[h], wbuf.at[h], wx_s.at[h], wx_r.at[h], partner)
-    for load in loads:
-        load.start()
     rate_col[...] = jnp.transpose(jnp.broadcast_to(rates[...], (TILE, TOK)))
 
     @pl.loop(0, TOK // 256)
@@ -313,7 +309,13 @@
         x_it[...] = (g * (1.0 / (size + 1e-06))).astype(BF16)
 
     def iterate():
-        gram[...] = dot(x_it[...], x_it[...], 1, 1).astype(BF16)
+        for low in (0, 256, 512):
+            high = min(low + 256, HD)
+            cols = pl.ds(low, high - low)
+            strip = dot(x_it[pl.ds(low, HD - low), :], x_it[cols, :], 1, 1).astype(BF16)
+            gram[pl.ds(low, HD - low), cols] = strip
+            if high < HD:
+                gram[cols, pl.ds(high, HD - high)] = jnp.transpose(strip[high - low:, :])
         prod[...] = dot(gram[...], x_it[...]).astype(BF16)
         second = dot(gram[...], prod[...])
         x_it[...] = (
@@ -360,6 +362,10 @@
     halo_begin(1)
     halo_half(1, 0)
     halo_half(1, 1)
+    for h in range(2 * NX):
+        go(weight.at[h], wbuf.at[h], wx_s.at[h], wx_r.at[h], partner)
+    for load in loads:
+        load.start()
     weights_of(1, 0, 3)
     ag_step(0, 1)
     weights_of(1, 3, 5)

time: 123 us -> 120 us (0.976)
  Pallas kernels: 121 us -> 118 us
    pallas_call x1, Pallas kernels: 121 us -> 118 us  [layer(): pl.pallas_call(layer_kernel, name='layer', out_shape=jax.ShapeDtypeStruct...]
where the time goes in v3:
time: 120 us
  Pallas kernels  118 us (98%)
  local copies, waits for them, and re-layouts  1.98 us (2%)
    pallas_call x1, Pallas kernels, layer(): pl.pallas_call(layer_kernel, name='layer', out_shape=jax.ShapeDtypeStruct...  118 us

profile of v3, /device:TPU:1, one launch (start us, length us, event | category | flops | bytes accessed | tf_op | source)
XLA Modules:
  0.0 119.5 jit_solution(1121386590275504487)
XLA Ops:
  0.0 117.5 %layer.1 = bf16[512,640]{1,0:T(8,128)(2,1)} custom-call(bf16[512,640]{1,0:T(8,128)(2,1)} %q.1, bf16[512,640]{1,0:T(8,128)(2,1)} %k.1, bf16[512,640]{1,0:T(8,128)(2,1)} %v.1, f32[1,512]{1,0:T(1,128)} %rates.1, bf16[640,640]{1,0:T(8,128)(2,1)} %bitcast.5, bf16[640,640]{1,0:T(8,128)(2,1)} %bitcast.6, bf16[640,640]{1,0:T(8,128)(2,1)} %bitcast.7, f32[640]{0:T(1024)} %gain.1, ...), custom_call_target="tpu_custom_call" | custom-call | tf_op jit(solution)/shard_map/layer/pallas_call | solution.py:506
  117.5 2.0 %copy.11 = bf16[512,640]{1,0:T(8,128)(2,1)} copy(bf16[512,640]{1,0:T(8,128)(2,1)} %layer.1) | data formatting | bytes 1310720
